TPU v7x, 128 devices: a whole 4x4x4 slice. The times are simulated.
128 devices in a mesh: ctx: 32 (over z, x_hi, y), tp: 4 (over x_lo, core).
Axes of the slice: x: 4 (x_hi: 2, x_lo: 2; x = x_hi * 2 + x_lo), y: 4, z: 4, core: 2. Of those that a mesh axis runs over, the one named last changes fastest.
Arguments:
- queries: bfloat16 [16384, 4096], P('ctx', 'tp'), may hold values from -6 to 6
- keys: bfloat16 [16384, 512], P('ctx', 'tp'), may hold values from -6 to 6
- values: bfloat16 [16384, 512], P('ctx', 'tp'), may hold values from -6 to 6
- out_weight: bfloat16 [4096, 8192], P('tp'), may hold values from -0.75 to 0.75
- vertical: int32 [32, 16], P('tp'), may hold values from 0 to 255, as said below
- slash: int32 [32, 8], P('tp'), may hold values from 0 to 15, as said below
Outputs:
- projected: bfloat16 [16384, 8192], P(('ctx', 'tp'))
Inputs may be any that keep to these rules, and one draw needn't show every extreme that they name: `vertical`: each head's 16 blocks are distinct. For each index of tp, the blocks named by its 8 heads include at most 2 blocks of any one ctx shard of 512 tokens, and exactly 2 of some shard. `slash`: each head's first offset is 0 and its 8 offsets are distinct.
All inputs are finite; a program needn't handle non-finite values.
Results may differ from a plain program's by a relative error of at most 0.013.
Values may be sent and summed in bfloat16 or wider, within the bound.
A program may use at most 128 MiB of HBM per device.

v0:
```python
import jax
import jax.numpy as jnp
from jax import lax
from jax.sharding import PartitionSpec as P

HS = 128
BLK = 64


def slot_table(vert_row, slash_row, query_blocks):
    block_count = query_blocks.shape[0]
    column_ids = query_blocks[:, None]
    vert_blocks = jnp.broadcast_to(vert_row[None, :], (block_count, vert_row.shape[0]))
    vert_ok = vert_blocks <= column_ids
    slash_blocks = column_ids - slash_row[None, :]
    repeated = jnp.any(slash_blocks[:, :, None] == vert_row[None, None, :], axis=2)
    slash_ok = (slash_blocks >= 0) & jnp.logical_not(repeated)
    blocks = jnp.concatenate([vert_blocks, slash_blocks], axis=1)
    usable = jnp.concatenate([vert_ok, slash_ok], axis=1)
    return (blocks, usable)


def attend(head_query, key_tiles, value_tiles, blocks, usable, query_blocks):
    block_len = head_query.shape[1]
    score_scale = 1.0 / jnp.sqrt(jnp.float32(head_query.shape[2]))
    scores = (
        jnp.einsum("ibd,isjd->ibsj", head_query, key_tiles, preferred_element_type=jnp.float32)
        * score_scale
    )
    diagonal = blocks == query_blocks[:, None]
    positions = jnp.arange(block_len, dtype=jnp.int32)
    above_diag = positions[None, :] > positions[:, None]
    blocked = (
        jnp.logical_not(usable)[:, None, :, None]
        | diagonal[:, None, :, None] & above_diag[None, :, None, :]
    )
    scores = jnp.where(blocked, jnp.float32(-1e30), scores)
    row_max = jnp.max(scores, axis=(2, 3), keepdims=True)
    weights = jnp.exp(scores - row_max)
    row_total = jnp.sum(weights, axis=(2, 3))
    rounded_probs = weights.astype(jnp.bfloat16)
    attended = jnp.einsum(
        "ibsj,isjd->ibd", rounded_probs, value_tiles, preferred_element_type=jnp.float32
    )
    return (attended / row_total[:, :, None]).astype(jnp.bfloat16)


def shards(queries, keys, values, out_weight, vertical, slash):
    local_rows = queries.shape[0]
    local_heads = vertical.shape[0]
    local_blocks = local_rows // BLK
    ctx_rank = lax.axis_index("ctx")
    keyvals = jnp.concatenate([keys, values], axis=1).reshape(local_blocks, BLK, 2 * HS)
    first_block = ctx_rank * local_blocks
    query_blocks = first_block + jnp.arange(local_blocks, dtype=jnp.int32)
    source = lax.all_gather(keyvals, "ctx", axis=0, tiled=True)

    def locate(blocks):
        return jnp.clip(blocks, 0, source.shape[0] - 1)

    head_queries = queries.reshape(local_blocks, BLK, local_heads, HS).transpose(2, 0, 1, 3)

    def one_head(inputs):
        head_query, vert_row, slash_row = inputs
        blocks, usable = slot_table(vert_row, slash_row, query_blocks)
        chosen = source[locate(blocks)]
        return attend(head_query, chosen[..., :HS], chosen[..., HS:], blocks, usable, query_blocks)

    heads_out = lax.map(one_head, (head_queries, vertical, slash))
    attended = heads_out.transpose(1, 2, 0, 3).reshape(local_rows, local_heads * HS)
    product = jnp.dot(attended, out_weight, preferred_element_type=jnp.float32)
    return lax.psum_scatter(
        lax.optimization_barrier(product.astype(jnp.bfloat16))
        .astype(jnp.float32)
        .astype(jnp.bfloat16),
        "tp",
        scatter_dimension=0,
        tiled=True,
    )


def solution(mesh):
    return jax.shard_map(
        shards,
        mesh=mesh,
        in_specs=(
            P("ctx", "tp"),
            P("ctx", "tp"),
            P("ctx", "tp"),
            P("tp", None),
            P("tp", None),
            P("tp", None),
        ),
        out_specs=P(("ctx", "tp"), None),
        check_vma=False,
    )
```

profile of v0, /device:TPU:1, one launch (start us, length us, event | category | flops | bytes accessed | tf_op | source)
XLA Modules:
  0.0 411.1 jit_solution(11067707473191889496)
XLA Ops:
  10.2 107.0 %all-gather.2.cloned.1.call-done = bf16[256,64,256]{2,1,0:T(8,128)(2,1)} async-done(((bf16[8,64,256]{2,1,0:T(8,128)(2,1)}), bf16[256,64,256]{2,1,0:T(8,128)(2,1)}) %all-gather.2.cloned.1.call-update) | async-done | bytes 8388624 | tf_op jit(solution)/shard_map/all_gather | solution.py:56
  117.2 191.7 %while.11 = (s32[]{:T(128)}, bf16[8,8,64,128]{3,2,1,0:T(8,128)(2,1)S(1)}, s32[8,16]{1,0:T(8,128)}, s32[8,8]{1,0:T(8,128)}, bf16[8,8,64,128]{3,2,1,0:T(8,128)(2,1...) while((s32[]{:T(128)}, bf16[8,8,64,128]{3,2,1,0:T(8,128)(2,1)S(1)}, ...), condition=%wide.region_4.5_spmd.clone, body=%wide.region_0.4_spmd.clone.sunk | while | flops 416161856 | bytes 50649856 | solution.py:69
  119.4 11.5 %gather_fusion = bf16[192,64,256]{2,1,0:T(8,128)(2,1)} fusion(bf16[256,64,256]{2,1,0:T(8,128)(2,1)} %get-tuple-element.179, s32[1024]{0:T(1024)S(1)} %pad_clamp_fusion.2), kind=kCustom, calls=%fused_computation.clone.clone.1 | custom fusion | bytes 12583680 | tf_op jit(solution)/shard_map/while/body/eval_jaxpr/gather | solution.py:66
  130.9 4.4 %fusion.61 = (f32[8,64]{1,0:T(8,128)S(1)}, f32[8,64,24,64]{1,3,2,0:T(8,128)S(1)}) fusion(pred[64,64]{0,1:T(8,128)(4,1)S(1)} %iota_compare_fusion.2, pred[8,24]{1,0:T(8,128)(4,1)S(1)} %get-tuple-element.152, pred[8,24]{1,0:T(8,128)(4,1)S(1)} %get-tuple-element.153, bf16[8,24,64,256]{3,2,1,0:T(8,128)(2,1)} %bitcast.59, ...), kind=kOutput, calls=%fused_computation.6.clone.1 | convolution fusion | flops 205258240 | bytes 6435328 | tf_op jit(solution)/shard_map/while/body/eval_jaxpr/ibd,isjd->ibsj/dot_general | solution.py:27
  137.8 3.4 fusion.63
  143.3 11.5 %gather_fusion = bf16[192,64,256]{2,1,0:T(8,128)(2,1)} fusion(bf16[256,64,256]{2,1,0:T(8,128)(2,1)} %get-tuple-element.179, s32[1024]{0:T(1024)S(1)} %pad_clamp_fusion.2), kind=kCustom, calls=%fused_computation.clone.clone.1 | custom fusion | bytes 12583680 | tf_op jit(solution)/shard_map/while/body/eval_jaxpr/gather | solution.py:66
  154.8 4.4 %fusion.61 = (f32[8,64]{1,0:T(8,128)S(1)}, f32[8,64,24,64]{1,3,2,0:T(8,128)S(1)}) fusion(pred[64,64]{0,1:T(8,128)(4,1)S(1)} %iota_compare_fusion.2, pred[8,24]{1,0:T(8,128)(4,1)S(1)} %get-tuple-element.152, pred[8,24]{1,0:T(8,128)(4,1)S(1)} %get-tuple-element.153, bf16[8,24,64,256]{3,2,1,0:T(8,128)(2,1)} %bitcast.59, ...), kind=kOutput, calls=%fused_computation.6.clone.1 | convolution fusion | flops 205258240 | bytes 6435328 | tf_op jit(solution)/shard_map/while/body/eval_jaxpr/ibd,isjd->ibsj/dot_general | solution.py:27
  167.3 11.5 %gather_fusion = bf16[192,64,256]{2,1,0:T(8,128)(2,1)} fusion(bf16[256,64,256]{2,1,0:T(8,128)(2,1)} %get-tuple-element.179, s32[1024]{0:T(1024)S(1)} %pad_clamp_fusion.2), kind=kCustom, calls=%fused_computation.clone.clone.1 | custom fusion | bytes 12583680 | tf_op jit(solution)/shard_map/while/body/eval_jaxpr/gather | solution.py:66
  178.8 4.4 %fusion.61 = (f32[8,64]{1,0:T(8,128)S(1)}, f32[8,64,24,64]{1,3,2,0:T(8,128)S(1)}) fusion(pred[64,64]{0,1:T(8,128)(4,1)S(1)} %iota_compare_fusion.2, pred[8,24]{1,0:T(8,128)(4,1)S(1)} %get-tuple-element.152, pred[8,24]{1,0:T(8,128)(4,1)S(1)} %get-tuple-element.153, bf16[8,24,64,256]{3,2,1,0:T(8,128)(2,1)} %bitcast.59, ...), kind=kOutput, calls=%fused_computation.6.clone.1 | convolution fusion | flops 205258240 | bytes 6435328 | tf_op jit(solution)/shard_map/while/body/eval_jaxpr/ibd,isjd->ibsj/dot_general | solution.py:27
  191.2 11.5 %gather_fusion = bf16[192,64,256]{2,1,0:T(8,128)(2,1)} fusion(bf16[256,64,256]{2,1,0:T(8,128)(2,1)} %get-tuple-element.179, s32[1024]{0:T(1024)S(1)} %pad_clamp_fusion.2), kind=kCustom, calls=%fused_computation.clone.clone.1 | custom fusion | bytes 12583680 | tf_op jit(solution)/shard_map/while/body/eval_jaxpr/gather | solution.py:66
  202.8 4.4 %fusion.61 = (f32[8,64]{1,0:T(8,128)S(1)}, f32[8,64,24,64]{1,3,2,0:T(8,128)S(1)}) fusion(pred[64,64]{0,1:T(8,128)(4,1)S(1)} %iota_compare_fusion.2, pred[8,24]{1,0:T(8,128)(4,1)S(1)} %get-tuple-element.152, pred[8,24]{1,0:T(8,128)(4,1)S(1)} %get-tuple-element.153, bf16[8,24,64,256]{3,2,1,0:T(8,128)(2,1)} %bitcast.59, ...), kind=kOutput, calls=%fused_computation.6.clone.1 | convolution fusion | flops 205258240 | bytes 6435328 | tf_op jit(solution)/shard_map/while/body/eval_jaxpr/ibd,isjd->ibsj/dot_general | solution.py:27
  209.7 3.4 fusion.63
  215.2 11.5 %gather_fusion = bf16[192,64,256]{2,1,0:T(8,128)(2,1)} fusion(bf16[256,64,256]{2,1,0:T(8,128)(2,1)} %get-tuple-element.179, s32[1024]{0:T(1024)S(1)} %pad_clamp_fusion.2), kind=kCustom, calls=%fused_computation.clone.clone.1 | custom fusion | bytes 12583680 | tf_op jit(solution)/shard_map/while/body/eval_jaxpr/gather | solution.py:66
  226.7 4.4 %fusion.61 = (f32[8,64]{1,0:T(8,128)S(1)}, f32[8,64,24,64]{1,3,2,0:T(8,128)S(1)}) fusion(pred[64,64]{0,1:T(8,128)(4,1)S(1)} %iota_compare_fusion.2, pred[8,24]{1,0:T(8,128)(4,1)S(1)} %get-tuple-element.152, pred[8,24]{1,0:T(8,128)(4,1)S(1)} %get-tuple-element.153, bf16[8,24,64,256]{3,2,1,0:T(8,128)(2,1)} %bitcast.59, ...), kind=kOutput, calls=%fused_computation.6.clone.1 | convolution fusion | flops 205258240 | bytes 6435328 | tf_op jit(solution)/shard_map/while/body/eval_jaxpr/ibd,isjd->ibsj/dot_general | solution.py:27
  233.6 3.4 fusion.63
  239.2 11.5 %gather_fusion = bf16[192,64,256]{2,1,0:T(8,128)(2,1)} fusion(bf16[256,64,256]{2,1,0:T(8,128)(2,1)} %get-tuple-element.179, s32[1024]{0:T(1024)S(1)} %pad_clamp_fusion.2), kind=kCustom, calls=%fused_computation.clone.clone.1 | custom fusion | bytes 12583680 | tf_op jit(solution)/shard_map/while/body/eval_jaxpr/gather | solution.py:66
  250.7 4.4 %fusion.61 = (f32[8,64]{1,0:T(8,128)S(1)}, f32[8,64,24,64]{1,3,2,0:T(8,128)S(1)}) fusion(pred[64,64]{0,1:T(8,128)(4,1)S(1)} %iota_compare_fusion.2, pred[8,24]{1,0:T(8,128)(4,1)S(1)} %get-tuple-element.152, pred[8,24]{1,0:T(8,128)(4,1)S(1)} %get-tuple-element.153, bf16[8,24,64,256]{3,2,1,0:T(8,128)(2,1)} %bitcast.59, ...), kind=kOutput, calls=%fused_computation.6.clone.1 | convolution fusion | flops 205258240 | bytes 6435328 | tf_op jit(solution)/shard_map/while/body/eval_jaxpr/ibd,isjd->ibsj/dot_general | solution.py:27
  263.1 11.5 %gather_fusion = bf16[192,64,256]{2,1,0:T(8,128)(2,1)} fusion(bf16[256,64,256]{2,1,0:T(8,128)(2,1)} %get-tuple-element.179, s32[1024]{0:T(1024)S(1)} %pad_clamp_fusion.2), kind=kCustom, calls=%fused_computation.clone.clone.1 | custom fusion | bytes 12583680 | tf_op jit(solution)/shard_map/while/body/eval_jaxpr/gather | solution.py:66
  274.6 4.4 %fusion.61 = (f32[8,64]{1,0:T(8,128)S(1)}, f32[8,64,24,64]{1,3,2,0:T(8,128)S(1)}) fusion(pred[64,64]{0,1:T(8,128)(4,1)S(1)} %iota_compare_fusion.2, pred[8,24]{1,0:T(8,128)(4,1)S(1)} %get-tuple-element.152, pred[8,24]{1,0:T(8,128)(4,1)S(1)} %get-tuple-element.153, bf16[8,24,64,256]{3,2,1,0:T(8,128)(2,1)} %bitcast.59, ...), kind=kOutput, calls=%fused_computation.6.clone.1 | convolution fusion | flops 205258240 | bytes 6435328 | tf_op jit(solution)/shard_map/while/body/eval_jaxpr/ibd,isjd->ibsj/dot_general | solution.py:27
  281.5 3.4 fusion.63
  287.1 11.5 %gather_fusion = bf16[192,64,256]{2,1,0:T(8,128)(2,1)} fusion(bf16[256,64,256]{2,1,0:T(8,128)(2,1)} %get-tuple-element.179, s32[1024]{0:T(1024)S(1)} %pad_clamp_fusion.2), kind=kCustom, calls=%fused_computation.clone.clone.1 | custom fusion | bytes 12583680 | tf_op jit(solution)/shard_map/while/body/eval_jaxpr/gather | solution.py:66
  298.6 4.4 %fusion.61 = (f32[8,64]{1,0:T(8,128)S(1)}, f32[8,64,24,64]{1,3,2,0:T(8,128)S(1)}) fusion(pred[64,64]{0,1:T(8,128)(4,1)S(1)} %iota_compare_fusion.2, pred[8,24]{1,0:T(8,128)(4,1)S(1)} %get-tuple-element.152, pred[8,24]{1,0:T(8,128)(4,1)S(1)} %get-tuple-element.153, bf16[8,24,64,256]{3,2,1,0:T(8,128)(2,1)} %bitcast.59, ...), kind=kOutput, calls=%fused_computation.6.clone.1 | convolution fusion | flops 205258240 | bytes 6435328 | tf_op jit(solution)/shard_map/while/body/eval_jaxpr/ibd,isjd->ibsj/dot_general | solution.py:27
  309.6 16.8 %convolution_convert_fusion = bf16[512,8192]{1,0:T(8,128)(2,1)} fusion(bf16[1024,8192]{1,0:T(8,128)(2,1)} %param.11, bf16[64,8,8,128]{3,2,1,0:T(8,128)(2,1)S(1)} %bitcast.66), kind=kOutput, calls=%fused_computation.42 | convolution fusion | flops 8594128896 | bytes 26214400 | tf_op jit(solution)/shard_map/dot_general | solution.py:71
  326.4 77.8 %reduce-scatter.2.cloned.1.call-done = bf16[128,8192]{1,0:T(8,128)(2,1)} async-done(((bf16[512,8192]{1,0:T(8,128)(2,1)}), bf16[128,8192]{1,0:T(8,128)(2,1)}) %reduce-scatter.2.cloned.1.call-update) | async-done | bytes 2097168 | tf_op jit(solution)/shard_map/reduce_scatter | solution.py:72
  (174 shorter events, 54.9 us)
Async XLA Ops:
  6.5 110.7 %all-gather.2.cloned.1.call-start = ((), (), s32[]{:S(2)}) async-start(), calls=%async_computation.1 | async-start | bytes 8650752 | tf_op jit(solution)/shard_map/all_gather | solution.py:56
  8.3 396.0 %reduce-scatter.2.cloned.1.call-start = ((), (), s32[]{:S(2)}) async-start(), calls=%async_computation.2 | async-start | bytes 10485760 | tf_op jit(solution)/shard_map/reduce_scatter | solution.py:72
  130.9 6.9 %slice-start = ((s8[6291456]{0:T(1024)(128)(4,1)}), s8[4194304]{0:T(1024)(128)(4,1)S(1)}, s32[]{:S(2)}) async-start(s8[6291456]{0:T(1024)(128)(4,1)} %bitcast.60), calls=%async_computation.3 | async-start | bytes 8388608 | tf_op jit(solution)/shard_map/while
  130.9 6.9 %slice-start.1 = ((s8[6291456]{0:T(1024)(128)(4,1)}), s8[2097152]{0:T(1024)(128)(4,1)S(1)}, s32[]{:S(2)}) async-start(s8[6291456]{0:T(1024)(128)(4,1)} %bitcast.60), calls=%async_computation.4 | async-start | bytes 4194304 | tf_op jit(solution)/shard_map/while
  154.8 6.9 %slice-start = ((s8[6291456]{0:T(1024)(128)(4,1)}), s8[4194304]{0:T(1024)(128)(4,1)S(1)}, s32[]{:S(2)}) async-start(s8[6291456]{0:T(1024)(128)(4,1)} %bitcast.60), calls=%async_computation.3 | async-start | bytes 8388608 | tf_op jit(solution)/shard_map/while
  154.8 6.9 %slice-start.1 = ((s8[6291456]{0:T(1024)(128)(4,1)}), s8[2097152]{0:T(1024)(128)(4,1)S(1)}, s32[]{:S(2)}) async-start(s8[6291456]{0:T(1024)(128)(4,1)} %bitcast.60), calls=%async_computation.4 | async-start | bytes 4194304 | tf_op jit(solution)/shard_map/while
  178.8 6.9 %slice-start = ((s8[6291456]{0:T(1024)(128)(4,1)}), s8[4194304]{0:T(1024)(128)(4,1)S(1)}, s32[]{:S(2)}) async-start(s8[6291456]{0:T(1024)(128)(4,1)} %bitcast.60), calls=%async_computation.3 | async-start | bytes 8388608 | tf_op jit(solution)/shard_map/while
  178.8 6.9 %slice-start.1 = ((s8[6291456]{0:T(1024)(128)(4,1)}), s8[2097152]{0:T(1024)(128)(4,1)S(1)}, s32[]{:S(2)}) async-start(s8[6291456]{0:T(1024)(128)(4,1)} %bitcast.60), calls=%async_computation.4 | async-start | bytes 4194304 | tf_op jit(solution)/shard_map/while
  202.7 6.9 %slice-start = ((s8[6291456]{0:T(1024)(128)(4,1)}), s8[4194304]{0:T(1024)(128)(4,1)S(1)}, s32[]{:S(2)}) async-start(s8[6291456]{0:T(1024)(128)(4,1)} %bitcast.60), calls=%async_computation.3 | async-start | bytes 8388608 | tf_op jit(solution)/shard_map/while
  202.8 6.9 %slice-start.1 = ((s8[6291456]{0:T(1024)(128)(4,1)}), s8[2097152]{0:T(1024)(128)(4,1)S(1)}, s32[]{:S(2)}) async-start(s8[6291456]{0:T(1024)(128)(4,1)} %bitcast.60), calls=%async_computation.4 | async-start | bytes 4194304 | tf_op jit(solution)/shard_map/while
  226.7 6.9 %slice-start = ((s8[6291456]{0:T(1024)(128)(4,1)}), s8[4194304]{0:T(1024)(128)(4,1)S(1)}, s32[]{:S(2)}) async-start(s8[6291456]{0:T(1024)(128)(4,1)} %bitcast.60), calls=%async_computation.3 | async-start | bytes 8388608 | tf_op jit(solution)/shard_map/while
  226.7 6.9 %slice-start.1 = ((s8[6291456]{0:T(1024)(128)(4,1)}), s8[2097152]{0:T(1024)(128)(4,1)S(1)}, s32[]{:S(2)}) async-start(s8[6291456]{0:T(1024)(128)(4,1)} %bitcast.60), calls=%async_computation.4 | async-start | bytes 4194304 | tf_op jit(solution)/shard_map/while
  250.7 6.9 %slice-start = ((s8[6291456]{0:T(1024)(128)(4,1)}), s8[4194304]{0:T(1024)(128)(4,1)S(1)}, s32[]{:S(2)}) async-start(s8[6291456]{0:T(1024)(128)(4,1)} %bitcast.60), calls=%async_computation.3 | async-start | bytes 8388608 | tf_op jit(solution)/shard_map/while
  250.7 6.9 %slice-start.1 = ((s8[6291456]{0:T(1024)(128)(4,1)}), s8[2097152]{0:T(1024)(128)(4,1)S(1)}, s32[]{:S(2)}) async-start(s8[6291456]{0:T(1024)(128)(4,1)} %bitcast.60), calls=%async_computation.4 | async-start | bytes 4194304 | tf_op jit(solution)/shard_map/while
  274.6 6.9 %slice-start = ((s8[6291456]{0:T(1024)(128)(4,1)}), s8[4194304]{0:T(1024)(128)(4,1)S(1)}, s32[]{:S(2)}) async-start(s8[6291456]{0:T(1024)(128)(4,1)} %bitcast.60), calls=%async_computation.3 | async-start | bytes 8388608 | tf_op jit(solution)/shard_map/while
  274.6 6.9 %slice-start.1 = ((s8[6291456]{0:T(1024)(128)(4,1)}), s8[2097152]{0:T(1024)(128)(4,1)S(1)}, s32[]{:S(2)}) async-start(s8[6291456]{0:T(1024)(128)(4,1)} %bitcast.60), calls=%async_computation.4 | async-start | bytes 4194304 | tf_op jit(solution)/shard_map/while
  298.6 6.9 %slice-start = ((s8[6291456]{0:T(1024)(128)(4,1)}), s8[4194304]{0:T(1024)(128)(4,1)S(1)}, s32[]{:S(2)}) async-start(s8[6291456]{0:T(1024)(128)(4,1)} %bitcast.60), calls=%async_computation.3 | async-start | bytes 8388608 | tf_op jit(solution)/shard_map/while
  298.6 6.9 %slice-start.1 = ((s8[6291456]{0:T(1024)(128)(4,1)}), s8[2097152]{0:T(1024)(128)(4,1)S(1)}, s32[]{:S(2)}) async-start(s8[6291456]{0:T(1024)(128)(4,1)} %bitcast.60), calls=%async_computation.4 | async-start | bytes 4194304 | tf_op jit(solution)/shard_map/while
Sparse Core Ops, SparseCore 0:
  10.5 106.6 all-gather.1
  326.6 77.6 reduce-scatter.1
where the time goes:
time: 412 us; the launch traced here: 411 us
  waiting for transfers between devices  185 us (45%)
  local copies, waits for them, and re-layouts  106 us (26%)
  matrix products  78.7 us (19%)
  other arithmetic  27 us (7%)
  between operations  13.5 us (3%)
    all_gather x1, waiting for transfers between devices, shards(): source = lax.all_gather(keyvals, 'ctx', axis=0, tiled=True)  107 us
    gather x8, local copies, waits for them, and re-layouts, one_head(): chosen = source[locate(blocks)]  91.8 us
    reduce_scatter x1, waiting for transfers between devices, shards(): lax.psum_scatter(lax.optimization_barrier(product.astype(jnp.bfloat16)).a...  77.8 us
    dot_general x8, matrix products, attend(): jnp.einsum('ibd,isjd->ibsj', head_query, key_tiles, preferred_element_typ...  35.1 us
    dot_general x8, matrix products, attend(): jnp.einsum('ibsj,isjd->ibd', rounded_probs, value_tiles, preferred_elemen...  26.8 us
    reduce_sum x8, other arithmetic, attend(): row_total = jnp.sum(weights, axis=(2, 3))  19.8 us
    dot_general x1, matrix products, shards(): product = jnp.dot(attended, out_weight, preferred_element_type=jnp.float32)  16.8 us
  transfers between devices with their start and end apart: 2, of which 2 were waited for; matrix products, arithmetic and copies ran while one was open for 0% of the time, Pallas kernels for 0%

commit v1 on v0

--- a/solution.py
+++ b/solution.py
@@ -53,7 +53,9 @@
     keyvals = jnp.concatenate([keys, values], axis=1).reshape(local_blocks, BLK, 2 * HS)
     first_block = ctx_rank * local_blocks
     query_blocks = first_block + jnp.arange(local_blocks, dtype=jnp.int32)
-    source = lax.all_gather(keyvals, "ctx", axis=0, tiled=True)
+    source = jnp.concatenate(
+        lax.all_to_all(jnp.stack([keyvals] * lax.axis_size("ctx")), "ctx", 0, 0), axis=0
+    )
 
     def locate(blocks):
         return jnp.clip(blocks, 0, source.shape[0] - 1)

time: 412 us -> 446 us (1.083)
  waiting for transfers between devices: 185 us -> 205 us
  starting transfers between devices: 0.04 us -> 11.6 us
    all_to_all x0 -> x1, waiting for transfers between devices: none -> 111 us  [shards(): lax.all_to_all(jnp.stack([keyvals] * lax.axis_size('ctx')), 'ctx', 0, 0)]
    all_gather x1 -> x0, waiting for transfers between devices: 107 us -> none  [shards(): source = lax.all_gather(keyvals, 'ctx', axis=0, tiled=True)]
    reduce_scatter x1, waiting for transfers between devices: 77.8 us -> 93.8 us  [shards(): lax.psum_scatter(lax.optimization_barrier(product.astype(jnp.bfloat16)).a...]
    all_to_all x0 -> x1, starting transfers between devices: none -> 11.6 us  [shards(): lax.all_to_all(jnp.stack([keyvals] * lax.axis_size('ctx')), 'ctx', 0, 0)]
where the time goes in v1:
time: 446 us; the launch traced here: 445 us
  waiting for transfers between devices  205 us (46%)
  local copies, waits for them, and re-layouts  109 us (24%)
  matrix products  78.8 us (18%)
  other arithmetic  26.3 us (6%)
  between operations  13.5 us (3%)
  starting transfers between devices  11.6 us (3%)
    all_to_all x1, waiting for transfers between devices, shards(): lax.all_to_all(jnp.stack([keyvals] * lax.axis_size('ctx')), 'ctx', 0, 0)  111 us
    reduce_scatter x1, waiting for transfers between devices, shards(): lax.psum_scatter(lax.optimization_barrier(product.astype(jnp.bfloat16)).a...  93.8 us
    gather x8, local copies, waits for them, and re-layouts, one_head(): chosen = source[locate(blocks)]  91.8 us
    dot_general x8, matrix products, attend(): jnp.einsum('ibd,isjd->ibsj', head_query, key_tiles, preferred_element_typ...  35.1 us
    dot_general x8, matrix products, attend(): jnp.einsum('ibsj,isjd->ibd', rounded_probs, value_tiles, preferred_elemen...  26.8 us
    reduce_sum x8, other arithmetic, attend(): row_total = jnp.sum(weights, axis=(2, 3))  19.8 us
    dot_general x1, matrix products, shards(): product = jnp.dot(attended, out_weight, preferred_element_type=jnp.float32)  16.8 us
    all_to_all x1, starting transfers between devices, shards(): lax.all_to_all(jnp.stack([keyvals] * lax.axis_size('ctx')), 'ctx', 0, 0)  11.6 us
  transfers between devices with their start and end apart: 2, of which 2 were waited for; matrix products, arithmetic and copies ran while one was open for 0% of the time, Pallas kernels for 0%

profile of v1, /device:TPU:1, one launch (start us, length us, event | category | flops | bytes accessed | tf_op | source)
XLA Modules:
  0.0 444.8 jit_solution(235820959232807907)
XLA Ops:
  7.5 4.3 stack.3
  11.8 11.6 %all-to-all-start = ((bf16[32,8,64,256]{3,2,1,0:T(8,128)(2,1)}), bf16[32,8,64,256]{3,2,1,0:T(8,128)(2,1)}, u32[]{:S(2)}, u32[]{:S(2)}) async-start(bf16[32,8,64,256]{3,2,1,0:T(8,128)(2,1)} %stack.3), calls=%async_computation | async-start | bytes 16777216 | tf_op jit(solution)/shard_map/all_to_all | solution.py:57
  24.1 110.8 %all-to-all-done = bf16[32,8,64,256]{3,2,1,0:T(8,128)(2,1)} async-done(((bf16[32,8,64,256]{3,2,1,0:T(8,128)(2,1)}), bf16[32,8,64,256]{3,2,1,0:T(8,128)(2,1)}, u32[]{:S(2)}, u32[]{:S(2)}) %all-to-all-start) | async-done | bytes 8388640 | tf_op jit(solution)/shard_map/all_to_all | solution.py:57
  135.0 191.7 %while.11 = (s32[]{:T(128)}, bf16[8,8,64,128]{3,2,1,0:T(8,128)(2,1)S(1)}, s32[8,16]{1,0:T(8,128)}, s32[8,8]{1,0:T(8,128)}, bf16[8,8,64,128]{3,2,1,0:T(8,128)(2,1...) while((s32[]{:T(128)}, bf16[8,8,64,128]{3,2,1,0:T(8,128)(2,1)S(1)}, ...), condition=%wide.region_4.5_spmd.clone, body=%wide.region_0.4_spmd.clone.sunk | while | flops 416161856 | bytes 50649856 | solution.py:71
  137.1 11.5 %gather_fusion = bf16[192,64,256]{2,1,0:T(8,128)(2,1)} fusion(bf16[256,64,256]{2,1,0:T(8,128)(2,1)} %get-tuple-element.172, s32[1024]{0:T(1024)S(1)} %pad_clamp_fusion.2), kind=kCustom, calls=%fused_computation.clone.clone.1 | custom fusion | bytes 12583680 | tf_op jit(solution)/shard_map/while/body/eval_jaxpr/gather | solution.py:68
  148.6 4.4 fusion.61
  161.1 11.5 %gather_fusion = bf16[192,64,256]{2,1,0:T(8,128)(2,1)} fusion(bf16[256,64,256]{2,1,0:T(8,128)(2,1)} %get-tuple-element.172, s32[1024]{0:T(1024)S(1)} %pad_clamp_fusion.2), kind=kCustom, calls=%fused_computation.clone.clone.1 | custom fusion | bytes 12583680 | tf_op jit(solution)/shard_map/while/body/eval_jaxpr/gather | solution.py:68
  172.6 4.4 fusion.61
  185.1 11.5 %gather_fusion = bf16[192,64,256]{2,1,0:T(8,128)(2,1)} fusion(bf16[256,64,256]{2,1,0:T(8,128)(2,1)} %get-tuple-element.172, s32[1024]{0:T(1024)S(1)} %pad_clamp_fusion.2), kind=kCustom, calls=%fused_computation.clone.clone.1 | custom fusion | bytes 12583680 | tf_op jit(solution)/shard_map/while/body/eval_jaxpr/gather | solution.py:68
  196.6 4.4 fusion.61
  203.5 3.4 fusion.63
  209.0 11.5 %gather_fusion = bf16[192,64,256]{2,1,0:T(8,128)(2,1)} fusion(bf16[256,64,256]{2,1,0:T(8,128)(2,1)} %get-tuple-element.172, s32[1024]{0:T(1024)S(1)} %pad_clamp_fusion.2), kind=kCustom, calls=%fused_computation.clone.clone.1 | custom fusion | bytes 12583680 | tf_op jit(solution)/shard_map/while/body/eval_jaxpr/gather | solution.py:68
  220.5 4.4 fusion.61
  227.4 3.4 fusion.63
  233.0 11.5 %gather_fusion = bf16[192,64,256]{2,1,0:T(8,128)(2,1)} fusion(bf16[256,64,256]{2,1,0:T(8,128)(2,1)} %get-tuple-element.172, s32[1024]{0:T(1024)S(1)} %pad_clamp_fusion.2), kind=kCustom, calls=%fused_computation.clone.clone.1 | custom fusion | bytes 12583680 | tf_op jit(solution)/shard_map/while/body/eval_jaxpr/gather | solution.py:68
  244.5 4.4 fusion.61
  256.9 11.5 %gather_fusion = bf16[192,64,256]{2,1,0:T(8,128)(2,1)} fusion(bf16[256,64,256]{2,1,0:T(8,128)(2,1)} %get-tuple-element.172, s32[1024]{0:T(1024)S(1)} %pad_clamp_fusion.2), kind=kCustom, calls=%fused_computation.clone.clone.1 | custom fusion | bytes 12583680 | tf_op jit(solution)/shard_map/while/body/eval_jaxpr/gather | solution.py:68
  268.4 4.4 fusion.61
  280.9 11.5 %gather_fusion = bf16[192,64,256]{2,1,0:T(8,128)(2,1)} fusion(bf16[256,64,256]{2,1,0:T(8,128)(2,1)} %get-tuple-element.172, s32[1024]{0:T(1024)S(1)} %pad_clamp_fusion.2), kind=kCustom, calls=%fused_computation.clone.clone.1 | custom fusion | bytes 12583680 | tf_op jit(solution)/shard_map/while/body/eval_jaxpr/gather | solution.py:68
  292.4 4.4 fusion.61
  304.9 11.5 %gather_fusion = bf16[192,64,256]{2,1,0:T(8,128)(2,1)} fusion(bf16[256,64,256]{2,1,0:T(8,128)(2,1)} %get-tuple-element.172, s32[1024]{0:T(1024)S(1)} %pad_clamp_fusion.2), kind=kCustom, calls=%fused_computation.clone.clone.1 | custom fusion | bytes 12583680 | tf_op jit(solution)/shard_map/while/body/eval_jaxpr/gather | solution.py:68
  316.4 4.4 fusion.61
  327.3 16.8 %convolution_convert_fusion = bf16[512,8192]{1,0:T(8,128)(2,1)} fusion(bf16[1024,8192]{1,0:T(8,128)(2,1)} %param.11, bf16[64,8,8,128]{3,2,1,0:T(8,128)(2,1)S(1)} %bitcast.68), kind=kOutput, calls=%fused_computation.42 | convolution fusion | flops 8594128896 | bytes 26214400 | tf_op jit(solution)/shard_map/dot_general | solution.py:73
  344.2 93.8 %reduce-scatter.2.cloned.1.call-done = bf16[128,8192]{1,0:T(8,128)(2,1)} async-done(((bf16[512,8192]{1,0:T(8,128)(2,1)}), bf16[128,8192]{1,0:T(8,128)(2,1)}) %reduce-scatter.2.cloned.1.call-update) | async-done | bytes 2097168 | tf_op jit(solution)/shard_map/reduce_scatter | solution.py:74
  (176 shorter events, 59.6 us)
Async XLA Ops:
  11.8 11.7 %copy-start = (bf16[512,1024]{1,0:T(8,128)(2,1)S(1)}, bf16[512,1024]{1,0:T(8,128)(2,1)}, u32[]{:S(2)}) copy-start(bf16[512,1024]{1,0:T(8,128)(2,1)} %param.8) | copy-start | bytes 3145732
  11.8 123.1 %all-to-all-start = ((bf16[32,8,64,256]{3,2,1,0:T(8,128)(2,1)}), bf16[32,8,64,256]{3,2,1,0:T(8,128)(2,1)}, u32[]{:S(2)}, u32[]{:S(2)}) async-start(bf16[32,8,64,256]{3,2,1,0:T(8,128)(2,1)} %stack.3), calls=%async_computation | async-start | bytes 16777216 | tf_op jit(solution)/shard_map/all_to_all | solution.py:57
  23.4 414.5 %reduce-scatter.2.cloned.1.call-start = ((), (), s32[]{:S(2)}) async-start(), calls=%async_computation.2 | async-start | bytes 10485760 | tf_op jit(solution)/shard_map/reduce_scatter | solution.py:74
  148.6 6.9 %slice-start = ((s8[6291456]{0:T(1024)(128)(4,1)}), s8[4194304]{0:T(1024)(128)(4,1)S(1)}, s32[]{:S(2)}) async-start(s8[6291456]{0:T(1024)(128)(4,1)} %bitcast.61), calls=%async_computation.3 | async-start | bytes 8388608 | tf_op jit(solution)/shard_map/while
  148.6 6.9 %slice-start.1 = ((s8[6291456]{0:T(1024)(128)(4,1)}), s8[2097152]{0:T(1024)(128)(4,1)S(1)}, s32[]{:S(2)}) async-start(s8[6291456]{0:T(1024)(128)(4,1)} %bitcast.61), calls=%async_computation.4 | async-start | bytes 4194304 | tf_op jit(solution)/shard_map/while
  172.6 6.9 %slice-start = ((s8[6291456]{0:T(1024)(128)(4,1)}), s8[4194304]{0:T(1024)(128)(4,1)S(1)}, s32[]{:S(2)}) async-start(s8[6291456]{0:T(1024)(128)(4,1)} %bitcast.61), calls=%async_computation.3 | async-start | bytes 8388608 | tf_op jit(solution)/shard_map/while
  172.6 6.9 %slice-start.1 = ((s8[6291456]{0:T(1024)(128)(4,1)}), s8[2097152]{0:T(1024)(128)(4,1)S(1)}, s32[]{:S(2)}) async-start(s8[6291456]{0:T(1024)(128)(4,1)} %bitcast.61), calls=%async_computation.4 | async-start | bytes 4194304 | tf_op jit(solution)/shard_map/while
  196.5 6.9 %slice-start = ((s8[6291456]{0:T(1024)(128)(4,1)}), s8[4194304]{0:T(1024)(128)(4,1)S(1)}, s32[]{:S(2)}) async-start(s8[6291456]{0:T(1024)(128)(4,1)} %bitcast.61), calls=%async_computation.3 | async-start | bytes 8388608 | tf_op jit(solution)/shard_map/while
  196.6 6.9 %slice-start.1 = ((s8[6291456]{0:T(1024)(128)(4,1)}), s8[2097152]{0:T(1024)(128)(4,1)S(1)}, s32[]{:S(2)}) async-start(s8[6291456]{0:T(1024)(128)(4,1)} %bitcast.61), calls=%async_computation.4 | async-start | bytes 4194304 | tf_op jit(solution)/shard_map/while
  220.5 6.9 %slice-start = ((s8[6291456]{0:T(1024)(128)(4,1)}), s8[4194304]{0:T(1024)(128)(4,1)S(1)}, s32[]{:S(2)}) async-start(s8[6291456]{0:T(1024)(128)(4,1)} %bitcast.61), calls=%async_computation.3 | async-start | bytes 8388608 | tf_op jit(solution)/shard_map/while
  220.5 6.9 %slice-start.1 = ((s8[6291456]{0:T(1024)(128)(4,1)}), s8[2097152]{0:T(1024)(128)(4,1)S(1)}, s32[]{:S(2)}) async-start(s8[6291456]{0:T(1024)(128)(4,1)} %bitcast.61), calls=%async_computation.4 | async-start | bytes 4194304 | tf_op jit(solution)/shard_map/while
  244.5 6.9 %slice-start = ((s8[6291456]{0:T(1024)(128)(4,1)}), s8[4194304]{0:T(1024)(128)(4,1)S(1)}, s32[]{:S(2)}) async-start(s8[6291456]{0:T(1024)(128)(4,1)} %bitcast.61), calls=%async_computation.3 | async-start | bytes 8388608 | tf_op jit(solution)/shard_map/while
  244.5 6.9 %slice-start.1 = ((s8[6291456]{0:T(1024)(128)(4,1)}), s8[2097152]{0:T(1024)(128)(4,1)S(1)}, s32[]{:S(2)}) async-start(s8[6291456]{0:T(1024)(128)(4,1)} %bitcast.61), calls=%async_computation.4 | async-start | bytes 4194304 | tf_op jit(solution)/shard_map/while
  268.4 6.9 %slice-start = ((s8[6291456]{0:T(1024)(128)(4,1)}), s8[4194304]{0:T(1024)(128)(4,1)S(1)}, s32[]{:S(2)}) async-start(s8[6291456]{0:T(1024)(128)(4,1)} %bitcast.61), calls=%async_computation.3 | async-start | bytes 8388608 | tf_op jit(solution)/shard_map/while
  268.4 6.9 %slice-start.1 = ((s8[6291456]{0:T(1024)(128)(4,1)}), s8[2097152]{0:T(1024)(128)(4,1)S(1)}, s32[]{:S(2)}) async-start(s8[6291456]{0:T(1024)(128)(4,1)} %bitcast.61), calls=%async_computation.4 | async-start | bytes 4194304 | tf_op jit(solution)/shard_map/while
  292.4 6.9 %slice-start = ((s8[6291456]{0:T(1024)(128)(4,1)}), s8[4194304]{0:T(1024)(128)(4,1)S(1)}, s32[]{:S(2)}) async-start(s8[6291456]{0:T(1024)(128)(4,1)} %bitcast.61), calls=%async_computation.3 | async-start | bytes 8388608 | tf_op jit(solution)/shard_map/while
  292.4 6.9 %slice-start.1 = ((s8[6291456]{0:T(1024)(128)(4,1)}), s8[2097152]{0:T(1024)(128)(4,1)S(1)}, s32[]{:S(2)}) async-start(s8[6291456]{0:T(1024)(128)(4,1)} %bitcast.61), calls=%async_computation.4 | async-start | bytes 4194304 | tf_op jit(solution)/shard_map/while
  316.4 6.9 %slice-start = ((s8[6291456]{0:T(1024)(128)(4,1)}), s8[4194304]{0:T(1024)(128)(4,1)S(1)}, s32[]{:S(2)}) async-start(s8[6291456]{0:T(1024)(128)(4,1)} %bitcast.61), calls=%async_computation.3 | async-start | bytes 8388608 | tf_op jit(solution)/shard_map/while
  316.4 6.9 %slice-start.1 = ((s8[6291456]{0:T(1024)(128)(4,1)}), s8[2097152]{0:T(1024)(128)(4,1)S(1)}, s32[]{:S(2)}) async-start(s8[6291456]{0:T(1024)(128)(4,1)} %bitcast.61), calls=%async_computation.4 | async-start | bytes 4194304 | tf_op jit(solution)/shard_map/while
Sparse Core Ops, SparseCore 0:
  344.3 93.5 reduce-scatter.1
